TPU v7x, 32 devices: a whole 2x2x4 slice. The times are simulated.
32 devices in a mesh: rows: 16 (over z, y, x), cols: 2 (over core).
Axes of the slice: x: 2, y: 2, z: 4, core: 2. Of those that a mesh axis runs over, the one named last changes fastest.
Arguments:
- slab: float32 [2048, 16384], P('rows', 'cols'), may hold values from -200 to 200, as said below
Outputs:
- r_rows: float32 [192, 16384], P(None, 'cols')
- updated: float32 [2048, 16384], P('rows', 'cols')
Inputs may be any that keep to these rules, and one draw needn't show every extreme that they name: `slab`: Real-valued activations; every panel has full column rank.
All inputs are finite; a program needn't handle non-finite values.
Results may differ from a plain program's by a relative error of at most 0.0003.
Values sent between devices are 32-bit elements; how exact they have to be, the bound alone decides.
No kernel may reach another device: no remote copies, remote signals or barrier semaphores. Data moves between devices by JAX's collectives and lax.ppermute only.
A program may use at most 64 MiB of HBM per device.

v0:
```python
import math
import jax
import jax.numpy as jnp
from jax import lax
from jax.sharding import PartitionSpec as P

PANEL = 64
PANELS = 3


def spread(value, axis, root):
    mine = lax.axis_index(axis) == root
    return lax.psum(jnp.where(mine, value, jnp.zeros_like(value)), axis)


def on_device(slab):
    rows_here = slab.shape[0]
    col_total = lax.axis_size("cols")
    norm_scale = 1.0 / math.sqrt(rows_here * lax.axis_size("rows"))
    current = slab
    blocks = []
    for turn in range(PANELS):
        owner_col = turn % col_total
        offset = turn // col_total * PANEL
        panel_cols = current[:, offset : offset + PANEL]
        shared = spread(panel_cols, "cols", owner_col)
        cross_terms = jnp.dot(shared.T, current, precision=lax.Precision.HIGHEST)
        gram_block = jnp.dot(shared.T, shared, precision=lax.Precision.HIGHEST)
        cross_terms, gram_block = lax.psum((cross_terms, gram_block), "rows")
        factor = jnp.linalg.cholesky(gram_block)
        coeffs = jax.scipy.linalg.solve_triangular(factor, cross_terms, lower=True)
        basis = jax.scipy.linalg.solve_triangular(factor, shared.T, lower=True).T
        current = current - jnp.dot(basis, coeffs, precision=lax.Precision.HIGHEST)
        blocks.append(coeffs * norm_scale)
    return (jnp.concatenate(blocks, 0), current)


def solution(mesh):
    placed = (P("rows", "cols"),)
    return jax.shard_map(
        on_device,
        mesh=mesh,
        in_specs=placed,
        out_specs=(P(None, "cols"), P("rows", "cols")),
        check_vma=False,
    )
```

profile of v0, /device:TPU:0, one launch (start us, length us, event | category | flops | bytes accessed | tf_op | source)
XLA Modules:
  0.0 459.2 jit_solution(14798924511112719745)
XLA Ops:
  7.2 0.0 all-reduce.4.cloned.1.call-start
  7.2 0.8 slice_select_fusion.2
  8.1 3.9 psum.63
  12.0 5.8 %fusion.22 = f32[64,8192]{1,0:T(8,128)} fusion(f32[128,64]{1,0:T(8,128)S(1)} %psum.63, f32[128,8192]{1,0:T(8,128)} %param.6), kind=kOutput, calls=%fused_computation.46 | convolution fusion | flops 805306368 | bytes 6324224 | tf_op jit(solution)/shard_map/dot_general | solution.py:27
  17.7 0.0 all-reduce.4.cloned.1.call-update
  17.8 0.0 all-reduce.6.cloned.1.call-start
  17.8 0.3 fusion.21
  18.1 79.4 %psum.64 = f32[64,64]{0,1:T(8,128)S(1)} all-reduce(f32[64,64]{0,1:T(8,128)S(1)} %fusion.21), channel_id=1, replica_groups=mesh['rows'=16,'cols'=2] {'rows'}, use_global_device_ids=true, to_apply=%region_1.2 | all-reduce | flops 4096 | bytes 32768 | tf_op jit(solution)/shard_map/psum | solution.py:29
  97.5 0.1 copy.4
  97.6 5.9 %cholesky.59 = f32[64,64]{1,0:T(8,128)S(1)} custom-call(f32[64,64]{1,0:T(8,128)S(1)} %fusion.20), custom_call_target="Cholesky" | custom-call | tf_op jit(solution)/shard_map/jit(cholesky)/cholesky | solution.py:30
  103.5 0.6 compare_reduce_fusion.2
  104.1 0.7 fusion.6
  104.8 4.9 %custom-call.12 = f32[1,64,64]{1,2,0:T(8,128)S(1)} custom-call(f32[1,64,64]{2,1,0:T(8,128)S(1)} %fusion.6), custom_call_target="InvertDiagBlocksLowerTriangular" | custom-call | tf_op jit(solution)/shard_map/jit(_solve_triangular)/triangular_solve | solution.py:31
  109.7 0.3 fusion.4
  110.0 37.9 %all-reduce.4.cloned.1.call-done = f32[64,8192]{1,0:T(8,128)} async-done(((f32[64,8192]{1,0:T(8,128)}), f32[64,8192]{1,0:T(8,128)}) %all-reduce.4.cloned.1.call-update) | async-done | bytes 2097168 | tf_op jit(solution)/shard_map/psum | solution.py:29
  147.9 3.7 broadcast_multiply_fusion.2
  151.5 3.6 convolution_subtract_fusion.2
  155.2 2.0 copy-done
  157.2 3.8 psum.66
  161.0 5.8 %fusion.24 = f32[64,8192]{1,0:T(8,128)} fusion(f32[128,64]{1,0:T(8,128)S(1)} %psum.66, f32[128,8192]{1,0:T(8,128)} %copy-done), kind=kOutput, calls=%fused_computation.48 | convolution fusion | flops 805306368 | bytes 6324224 | tf_op jit(solution)/shard_map/dot_general | solution.py:27
  166.8 0.0 all-reduce.8.cloned.1.call-start
  166.8 0.3 fusion.23
  167.1 76.0 %psum.67 = f32[64,64]{0,1:T(8,128)S(1)} all-reduce(f32[64,64]{0,1:T(8,128)S(1)} %fusion.23), channel_id=1, replica_groups=mesh['rows'=16,'cols'=2] {'rows'}, use_global_device_ids=true, to_apply=%region_6.10 | all-reduce | flops 4096 | bytes 32768 | tf_op jit(solution)/shard_map/psum | solution.py:29
  243.1 0.1 copy.6
  243.2 5.9 %cholesky.70 = f32[64,64]{1,0:T(8,128)S(1)} custom-call(f32[64,64]{1,0:T(8,128)S(1)} %fusion.16), custom_call_target="Cholesky" | custom-call | tf_op jit(solution)/shard_map/jit(cholesky)/cholesky | solution.py:30
  249.1 0.6 compare_reduce_fusion.1
  249.8 0.6 fusion.7
  250.4 4.9 %custom-call.14 = f32[1,64,64]{1,2,0:T(8,128)S(1)} custom-call(f32[1,64,64]{2,1,0:T(8,128)S(1)} %fusion.7), custom_call_target="InvertDiagBlocksLowerTriangular" | custom-call | tf_op jit(solution)/shard_map/jit(_solve_triangular)/triangular_solve | solution.py:31
  255.3 0.3 fusion.2
  255.6 37.9 %all-reduce.6.cloned.1.call-done = f32[64,8192]{1,0:T(8,128)} async-done(((f32[64,8192]{1,0:T(8,128)}), f32[64,8192]{1,0:T(8,128)}) %all-reduce.6.cloned.1.call-update) | async-done | bytes 2097168 | tf_op jit(solution)/shard_map/psum | solution.py:29
  293.5 5.0 %broadcast_multiply_fusion.1 = (f32[64,8192]{1,0:T(8,128)}, f32[64,8192]{1,0:T(8,128)S(1)}) fusion(f32[64,8192]{1,0:T(8,128)} %all-reduce.6.cloned.1.call-done, f32[1,64,64]{1,2,0:T(8,128)S(1)} %custom-call.14), kind=kOutput, calls=%fused_computation.5 | convolution fusion | flops 403177472 | bytes 6307840 | tf_op jit(solution)/shard_map/jit(_solve_triangular)/triangular_solve | solution.py:31
  298.5 3.6 convolution_subtract_fusion.1
  302.1 2.0 copy-done.2
  304.1 0.1 slice_select_fusion
  304.2 3.8 psum.69
  308.0 5.8 %fusion.26 = f32[64,8192]{1,0:T(8,128)} fusion(f32[128,64]{1,0:T(8,128)S(1)} %psum.69, f32[128,8192]{1,0:T(8,128)} %copy-done.2), kind=kOutput, calls=%fused_computation.50 | convolution fusion | flops 805306368 | bytes 6324224 | tf_op jit(solution)/shard_map/dot_general | solution.py:27
  313.8 0.3 fusion.25
  314.1 76.2 %psum.70 = f32[64,64]{0,1:T(8,128)S(1)} all-reduce(f32[64,64]{0,1:T(8,128)S(1)} %fusion.25), channel_id=1, replica_groups=mesh['rows'=16,'cols'=2] {'rows'}, use_global_device_ids=true, to_apply=%region_9.13 | all-reduce | flops 4096 | bytes 32768 | tf_op jit(solution)/shard_map/psum | solution.py:29
  390.3 0.1 copy.8
  390.4 5.8 %cholesky.81 = f32[64,64]{1,0:T(8,128)S(1)} custom-call(f32[64,64]{1,0:T(8,128)S(1)} %fusion.12), custom_call_target="Cholesky" | custom-call | tf_op jit(solution)/shard_map/jit(cholesky)/cholesky | solution.py:30
  396.2 0.6 compare_reduce_fusion
  396.9 0.6 fusion.8
  397.5 4.9 %custom-call.16 = f32[1,64,64]{1,2,0:T(8,128)S(1)} custom-call(f32[1,64,64]{2,1,0:T(8,128)S(1)} %fusion.8), custom_call_target="InvertDiagBlocksLowerTriangular" | custom-call | tf_op jit(solution)/shard_map/jit(_solve_triangular)/triangular_solve | solution.py:31
  402.4 0.3 fusion
  402.7 37.9 %all-reduce.8.cloned.1.call-done = f32[64,8192]{1,0:T(8,128)} async-done(((f32[64,8192]{1,0:T(8,128)}), f32[64,8192]{1,0:T(8,128)}) %all-reduce.8.cloned.1.call-update) | async-done | bytes 2097168 | tf_op jit(solution)/shard_map/psum | solution.py:29
  440.6 3.7 broadcast_multiply_fusion
  444.3 5.2 %convolution_subtract_fusion = f32[128,8192]{1,0:T(8,128)} fusion(f32[128,8192]{1,0:T(8,128)S(1)} %copy-done.3, f32[64,128]{1,0:T(8,128)S(1)} %fusion, f32[64,8192]{1,0:T(8,128)S(1)} %get-tuple-element.6), kind=kOutput, calls=%fused_computation | convolution fusion | flops 806354944 | bytes 10518528 | tf_op jit(solution)/shard_map/dot_general | solution.py:33
  449.5 3.1 pad_maximum_fusion
  (19 shorter events, 0.2 us)
Async XLA Ops:
  7.2 140.7 %all-reduce.4.cloned.1.call-start = ((), (), s32[]{:S(2)}) async-start(), calls=%async_computation | async-start | bytes 4194304 | tf_op jit(solution)/shard_map/psum | solution.py:29
  17.8 275.7 %all-reduce.6.cloned.1.call-start = ((), (), s32[]{:S(2)}) async-start(), calls=%async_computation.1 | async-start | bytes 4194304 | tf_op jit(solution)/shard_map/psum | solution.py:29
  147.9 3.7 copy-start.4
  155.2 2.0 copy-start
  166.8 273.8 %all-reduce.8.cloned.1.call-start = ((), (), s32[]{:S(2)}) async-start(), calls=%async_computation.2 | async-start | bytes 4194304 | tf_op jit(solution)/shard_map/psum | solution.py:29
  293.5 5.0 %copy-start.1 = (f32[128,8192]{1,0:T(8,128)S(1)}, f32[128,8192]{1,0:T(8,128)}, u32[]{:S(2)}) copy-start(f32[128,8192]{1,0:T(8,128)} %copy-done) | copy-start | bytes 12582916
  302.1 2.0 copy-start.2
  440.6 3.7 copy-start.3
  444.3 5.2 %copy-start.5 = (f32[64,8192]{1,0:T(8,128)S(1)}, f32[64,8192]{1,0:T(8,128)}, u32[]{:S(2)}) copy-start(f32[64,8192]{1,0:T(8,128)} %get-tuple-element.7) | copy-start | bytes 6291460
Sparse Core Ops, SparseCore 0:
  17.9 129.9 all-reduce.3
  166.9 126.5 all-reduce.5
  313.9 126.6 all-reduce.7
where the time goes:
time: 460 us; the launch traced here: 459 us
  blocking collectives  243 us (53%)
  waiting for transfers between devices  114 us (25%)
  matrix products  43.8 us (10%)
  other arithmetic  40.3 us (9%)
  between operations  14 us (3%)
    psum x3, blocking collectives, on_device(): cross_terms, gram_block = lax.psum((cross_terms, gram_block), 'rows')  232 us
    psum x3, waiting for transfers between devices, on_device(): cross_terms, gram_block = lax.psum((cross_terms, gram_block), 'rows')  114 us
    another operation x9, other arithmetic, on_device(): factor = jnp.linalg.cholesky(gram_block)  19.6 us
    dot_general x3, matrix products, on_device(): cross_terms = jnp.dot(shared.T, current, precision=lax.Precision.HIGHEST)  17.3 us
    another operation x6, other arithmetic, on_device(): coeffs = jax.scipy.linalg.solve_triangular(factor, cross_terms, lower=True)  16.6 us
    dot_general x3, matrix products, on_device(): current = current - jnp.dot(basis, coeffs, precision=lax.Precision.HIGHEST)  12.4 us
    another operation x3, matrix products, on_device(): coeffs = jax.scipy.linalg.solve_triangular(factor, cross_terms, lower=True)  12.4 us
    psum x3, blocking collectives, spread(): return lax.psum(jnp.where(mine, value, jnp.zeros_like(value)), axis)  11.5 us
  transfers between devices with their start and end apart: 3, of which 3 were waited for; matrix products, arithmetic and copies ran while one was open for 8% of the time, Pallas kernels for 0%

commit v1 on v0

--- a/solution.py
+++ b/solution.py
@@ -10,7 +10,7 @@
 
 def spread(value, axis, root):
     mine = lax.axis_index(axis) == root
-    return lax.psum(jnp.where(mine, value, jnp.zeros_like(value)), axis)
+    return jnp.sum(lax.all_gather(jnp.where(mine, value, jnp.zeros_like(value)), axis), axis=0)
 
 
 def on_device(slab):

time: 460 us -> 455 us (0.989)
  blocking collectives: 243 us -> 238 us
    psum x3 -> x0, blocking collectives: 11.5 us -> none  [spread(): return lax.psum(jnp.where(mine, value, jnp.zeros_like(value)), axis)]
    all_gather x0 -> x3, blocking collectives: none -> 6.23 us  [spread(): lax.all_gather(jnp.where(mine, value, jnp.zeros_like(value)), axis)]
where the time goes in v1:
time: 455 us; the launch traced here: 454 us
  blocking collectives  238 us (52%)
  waiting for transfers between devices  114 us (25%)
  matrix products  43.7 us (10%)
  other arithmetic  40.3 us (9%)
  between operations  14 us (3%)
    psum x3, blocking collectives, on_device(): cross_terms, gram_block = lax.psum((cross_terms, gram_block), 'rows')  232 us
    psum x3, waiting for transfers between devices, on_device(): cross_terms, gram_block = lax.psum((cross_terms, gram_block), 'rows')  114 us
    another operation x9, other arithmetic, on_device(): factor = jnp.linalg.cholesky(gram_block)  19.6 us
    dot_general x3, matrix products, on_device(): cross_terms = jnp.dot(shared.T, current, precision=lax.Precision.HIGHEST)  17.3 us
    another operation x6, other arithmetic, on_device(): coeffs = jax.scipy.linalg.solve_triangular(factor, cross_terms, lower=True)  16.6 us
    dot_general x3, matrix products, on_device(): current = current - jnp.dot(basis, coeffs, precision=lax.Precision.HIGHEST)  12.4 us
    another operation x3, matrix products, on_device(): coeffs = jax.scipy.linalg.solve_triangular(factor, cross_terms, lower=True)  12.4 us
  transfers between devices with their start and end apart: 3, of which 3 were waited for; matrix products, arithmetic and copies ran while one was open for 8% of the time, Pallas kernels for 0%

profile of v1, /device:TPU:0, one launch (start us, length us, event | category | flops | bytes accessed | tf_op | source)
XLA Modules:
  0.0 454.2 jit_solution(4521361623065282950)
XLA Ops:
  7.2 0.0 all-reduce.4.cloned.1.call-start
  7.2 0.8 slice_select_fusion.2
  8.1 2.0 all-gather
  10.1 5.8 %fusion.22 = f32[64,8192]{1,0:T(8,128)} fusion(f32[128,64]{1,0:T(8,128)S(1)} %reduce_sum.27, f32[128,8192]{1,0:T(8,128)} %param.6), kind=kOutput, calls=%fused_computation.46 | convolution fusion | flops 805306368 | bytes 6324224 | tf_op jit(solution)/shard_map/dot_general | solution.py:27
  15.9 0.0 all-reduce.4.cloned.1.call-update
  15.9 0.0 all-reduce.6.cloned.1.call-start
  16.0 0.3 fusion.21
  16.2 79.6 %psum.42 = f32[64,64]{0,1:T(8,128)S(1)} all-reduce(f32[64,64]{0,1:T(8,128)S(1)} %fusion.21), channel_id=1, replica_groups=mesh['rows'=16,'cols'=2] {'rows'}, use_global_device_ids=true, to_apply=%region_1.2 | all-reduce | flops 4096 | bytes 32768 | tf_op jit(solution)/shard_map/psum | solution.py:29
  95.8 0.1 copy.4
  95.9 5.9 %cholesky.59 = f32[64,64]{1,0:T(8,128)S(1)} custom-call(f32[64,64]{1,0:T(8,128)S(1)} %fusion.20), custom_call_target="Cholesky" | custom-call | tf_op jit(solution)/shard_map/jit(cholesky)/cholesky | solution.py:30
  101.8 0.6 compare_reduce_fusion.2
  102.5 0.7 fusion.6
  103.1 4.9 %custom-call.12 = f32[1,64,64]{1,2,0:T(8,128)S(1)} custom-call(f32[1,64,64]{2,1,0:T(8,128)S(1)} %fusion.6), custom_call_target="InvertDiagBlocksLowerTriangular" | custom-call | tf_op jit(solution)/shard_map/jit(_solve_triangular)/triangular_solve | solution.py:31
  108.0 0.3 fusion.4
  108.3 37.8 %all-reduce.4.cloned.1.call-done = f32[64,8192]{1,0:T(8,128)} async-done(((f32[64,8192]{1,0:T(8,128)}), f32[64,8192]{1,0:T(8,128)}) %all-reduce.4.cloned.1.call-update) | async-done | bytes 2097168 | tf_op jit(solution)/shard_map/psum | solution.py:29
  146.1 3.7 broadcast_multiply_fusion.2
  149.8 3.6 convolution_subtract_fusion.2
  153.4 2.0 copy-done
  155.5 2.1 all-gather.1
  157.6 5.8 %fusion.24 = f32[64,8192]{1,0:T(8,128)} fusion(f32[128,64]{1,0:T(8,128)S(1)} %reduce_sum.28, f32[128,8192]{1,0:T(8,128)} %copy-done), kind=kOutput, calls=%fused_computation.48 | convolution fusion | flops 805306368 | bytes 6324224 | tf_op jit(solution)/shard_map/dot_general | solution.py:27
  163.4 0.0 all-reduce.8.cloned.1.call-start
  163.4 0.3 fusion.23
  163.7 76.1 %psum.44 = f32[64,64]{0,1:T(8,128)S(1)} all-reduce(f32[64,64]{0,1:T(8,128)S(1)} %fusion.23), channel_id=1, replica_groups=mesh['rows'=16,'cols'=2] {'rows'}, use_global_device_ids=true, to_apply=%region_6.10 | all-reduce | flops 4096 | bytes 32768 | tf_op jit(solution)/shard_map/psum | solution.py:29
  239.8 0.1 copy.6
  239.9 5.9 %cholesky.70 = f32[64,64]{1,0:T(8,128)S(1)} custom-call(f32[64,64]{1,0:T(8,128)S(1)} %fusion.16), custom_call_target="Cholesky" | custom-call | tf_op jit(solution)/shard_map/jit(cholesky)/cholesky | solution.py:30
  245.8 0.6 compare_reduce_fusion.1
  246.4 0.6 fusion.7
  247.1 4.9 %custom-call.14 = f32[1,64,64]{1,2,0:T(8,128)S(1)} custom-call(f32[1,64,64]{2,1,0:T(8,128)S(1)} %fusion.7), custom_call_target="InvertDiagBlocksLowerTriangular" | custom-call | tf_op jit(solution)/shard_map/jit(_solve_triangular)/triangular_solve | solution.py:31
  252.0 0.3 fusion.2
  252.3 37.9 %all-reduce.6.cloned.1.call-done = f32[64,8192]{1,0:T(8,128)} async-done(((f32[64,8192]{1,0:T(8,128)}), f32[64,8192]{1,0:T(8,128)}) %all-reduce.6.cloned.1.call-update) | async-done | bytes 2097168 | tf_op jit(solution)/shard_map/psum | solution.py:29
  290.2 5.0 %broadcast_multiply_fusion.1 = (f32[64,8192]{1,0:T(8,128)}, f32[64,8192]{1,0:T(8,128)S(1)}) fusion(f32[64,8192]{1,0:T(8,128)} %all-reduce.6.cloned.1.call-done, f32[1,64,64]{1,2,0:T(8,128)S(1)} %custom-call.14), kind=kOutput, calls=%fused_computation.5 | convolution fusion | flops 403177472 | bytes 6307840 | tf_op jit(solution)/shard_map/jit(_solve_triangular)/triangular_solve | solution.py:31
  295.2 3.6 convolution_subtract_fusion.1
  298.8 2.0 copy-done.2
  300.8 0.1 slice_select_fusion
  300.9 2.1 all-gather.2
  303.0 5.8 %fusion.26 = f32[64,8192]{1,0:T(8,128)} fusion(f32[128,64]{1,0:T(8,128)S(1)} %reduce_sum.29, f32[128,8192]{1,0:T(8,128)} %copy-done.2), kind=kOutput, calls=%fused_computation.50 | convolution fusion | flops 805306368 | bytes 6324224 | tf_op jit(solution)/shard_map/dot_general | solution.py:27
  308.8 0.3 fusion.25
  309.1 76.2 %psum.46 = f32[64,64]{0,1:T(8,128)S(1)} all-reduce(f32[64,64]{0,1:T(8,128)S(1)} %fusion.25), channel_id=1, replica_groups=mesh['rows'=16,'cols'=2] {'rows'}, use_global_device_ids=true, to_apply=%region_9.13 | all-reduce | flops 4096 | bytes 32768 | tf_op jit(solution)/shard_map/psum | solution.py:29
  385.3 0.1 copy.8
  385.4 5.9 %cholesky.81 = f32[64,64]{1,0:T(8,128)S(1)} custom-call(f32[64,64]{1,0:T(8,128)S(1)} %fusion.12), custom_call_target="Cholesky" | custom-call | tf_op jit(solution)/shard_map/jit(cholesky)/cholesky | solution.py:30
  391.3 0.6 compare_reduce_fusion
  391.9 0.6 fusion.8
  392.5 4.9 %custom-call.16 = f32[1,64,64]{1,2,0:T(8,128)S(1)} custom-call(f32[1,64,64]{2,1,0:T(8,128)S(1)} %fusion.8), custom_call_target="InvertDiagBlocksLowerTriangular" | custom-call | tf_op jit(solution)/shard_map/jit(_solve_triangular)/triangular_solve | solution.py:31
  397.4 0.3 fusion
  397.7 37.9 %all-reduce.8.cloned.1.call-done = f32[64,8192]{1,0:T(8,128)} async-done(((f32[64,8192]{1,0:T(8,128)}), f32[64,8192]{1,0:T(8,128)}) %all-reduce.8.cloned.1.call-update) | async-done | bytes 2097168 | tf_op jit(solution)/shard_map/psum | solution.py:29
  435.6 3.7 broadcast_multiply_fusion
  439.3 5.2 %convolution_subtract_fusion = f32[128,8192]{1,0:T(8,128)} fusion(f32[128,8192]{1,0:T(8,128)S(1)} %copy-done.3, f32[64,128]{1,0:T(8,128)S(1)} %fusion, f32[64,8192]{1,0:T(8,128)S(1)} %get-tuple-element.6), kind=kOutput, calls=%fused_computation | convolution fusion | flops 806354944 | bytes 10518528 | tf_op jit(solution)/shard_map/dot_general | solution.py:33
  444.5 3.1 pad_maximum_fusion
  (22 shorter events, 0.2 us)
Async XLA Ops:
  7.2 139.0 %all-reduce.4.cloned.1.call-start = ((), (), s32[]{:S(2)}) async-start(), calls=%async_computation | async-start | bytes 4194304 | tf_op jit(solution)/shard_map/psum | solution.py:29
  15.9 274.2 %all-reduce.6.cloned.1.call-start = ((), (), s32[]{:S(2)}) async-start(), calls=%async_computation.1 | async-start | bytes 4194304 | tf_op jit(solution)/shard_map/psum | solution.py:29
  146.1 3.7 copy-start.4
  153.4 2.0 copy-start
  163.4 272.2 %all-reduce.8.cloned.1.call-start = ((), (), s32[]{:S(2)}) async-start(), calls=%async_computation.2 | async-start | bytes 4194304 | tf_op jit(solution)/shard_map/psum | solution.py:29
  290.2 5.0 %copy-start.1 = (f32[128,8192]{1,0:T(8,128)S(1)}, f32[128,8192]{1,0:T(8,128)}, u32[]{:S(2)}) copy-start(f32[128,8192]{1,0:T(8,128)} %copy-done) | copy-start | bytes 12582916
  298.8 2.0 copy-start.2
  435.6 3.7 copy-start.3
  439.3 5.2 %copy-start.5 = (f32[64,8192]{1,0:T(8,128)S(1)}, f32[64,8192]{1,0:T(8,128)}, u32[]{:S(2)}) copy-start(f32[64,8192]{1,0:T(8,128)} %get-tuple-element.7) | copy-start | bytes 6291460
Sparse Core Ops, SparseCore 0:
  16.0 130.0 all-reduce.3
  163.5 126.6 all-reduce.5
  308.9 126.6 all-reduce.7
